TPU v7x, 128 devices: a whole 4x4x4 slice. The times are simulated.
128 devices in a mesh: arc: 16 (over x, z), vec: 8 (over y, core).
Axes of the slice: x: 4, y: 4, z: 4, core: 2. Of those that a mesh axis runs over, the one named last changes fastest.
Arguments:
- right_side: float32 [640, 128, 128], P(('arc', 'vec')), may hold values from -6 to 6
- prior_diag: float32 [640, 128], P(('arc', 'vec')), may hold values from 0.5 to 4
- inv_factor: bfloat16 [2048, 256, 256], P(('arc', 'vec'))
- coupling_panel: bfloat16 [2048, 256, 1024], P(('arc', 'vec')), may hold values from -0.09375 to 0.09375
- coupling_owner: int32 [2048, 8], replicated, may hold values from 0 to 127, all different within a row; in each aligned block of 16 rows (0 to 15, 16 to 31, ...) at most 2 rows name the same one
- coupling_block: int32 [2048, 8], replicated, may hold values from 0 to 4
Outputs:
- solution_field: float32 [640, 128, 128], P(('arc', 'vec'))
- residual: float32 [640, 128, 128], P(('arc', 'vec'))
Inputs may be any that keep to these rules, and one draw needn't show every extreme that they name: `coupling_owner`: the 8 holders named for one arc are different. Among the 16 arcs of one device (aligned blocks of rows) no holder is named more than 2 times; some holder is named exactly 2 times.
All inputs are finite; a program needn't handle non-finite values.
Results may differ from a plain program's by a relative error of at most 0.006.
The roundings to bfloat16 on the way count: a program that leaves them out, or rounds other values in their place, can miss the bound.
Values may be sent and summed in bfloat16 or wider, within the bound.
A program may use at most 128 MiB of HBM per device.

v0:
```python
import jax
import jax.numpy as jnp
from jax import lax
from jax.sharding import PartitionSpec as P

ITERS = 2


def inner_gram(left, right):
    return jnp.einsum("grc,grd->cd", left, right, precision=lax.Precision.HIGHEST)


def combine_cols(field, weights):
    return jnp.einsum("grc,cd->grd", field, weights, precision=lax.Precision.HIGHEST)


def trade_out(buffer):
    return lax.all_to_all(buffer, ("arc", "vec"), split_axis=0, concat_axis=0, tiled=True)


def trade_back(buffer):
    return lax.all_to_all(buffer, ("arc", "vec"), split_axis=0, concat_axis=0, tiled=True)


def per_device(right_side, prior_diag, inv_factor, coupling_panel, coupling_owner, coupling_block):
    device_count = lax.axis_size(("arc", "vec"))
    my_index = lax.axis_index(("arc", "vec"))
    arcs_here = coupling_panel.shape[0]
    links = coupling_owner.shape[1]
    blocks_here = right_side.shape[0]
    block_rows = right_side.shape[1]
    rhs_count = right_side.shape[2]
    entries = arcs_here * links
    slot_count = (entries + device_count - 1) // device_count + 1
    owner_all = coupling_owner.reshape(device_count, entries)
    block_all = coupling_block.reshape(device_count, entries)
    position = jnp.arange(entries, dtype=jnp.int32)
    earlier = (owner_all[:, :, None] == owner_all[:, None, :]) & (
        position[None, None, :] < position[None, :, None]
    )
    rank_all = jnp.sum(earlier.astype(jnp.int32), axis=2)
    owner_mine = lax.dynamic_index_in_dim(owner_all, my_index, 0, keepdims=False)
    rank_mine = lax.dynamic_index_in_dim(rank_all, my_index, 0, keepdims=False)
    slot_mine = owner_mine * slot_count + rank_mine
    slot_ids = jnp.arange(slot_count, dtype=jnp.int32)
    matches = (owner_all[:, None, :] == my_index) & (
        rank_all[:, None, :] == slot_ids[None, :, None]
    )
    filled = jnp.any(matches, axis=2).reshape(-1)
    source_block = jnp.sum(jnp.where(matches, block_all[:, None, :], 0), axis=2).reshape(-1)
    block_ids = jnp.arange(blocks_here, dtype=jnp.int32)
    selector = ((source_block[:, None] == block_ids[None, :]) & filled[:, None]).astype(
        jnp.bfloat16
    )
    solution_field = jnp.zeros_like(right_side)
    residual = right_side
    direction = right_side
    res_gram = lax.psum(inner_gram(residual, residual), ("arc", "vec"))
    for sweep_index in range(ITERS):
        local_rounded = direction.astype(jnp.bfloat16)
        outgoing = jnp.where(
            filled[:, None, None], local_rounded[source_block], jnp.zeros((), jnp.bfloat16)
        )
        arrived = trade_out(outgoing)
        fetched = arrived[slot_mine].reshape(arcs_here, links * block_rows, rhs_count)
        coupled = jnp.einsum(
            "apk,akc->apc", coupling_panel, fetched, preferred_element_type=jnp.float32
        ).astype(jnp.bfloat16)
        whitened = jnp.einsum(
            "apq,aqc->apc", inv_factor, coupled, preferred_element_type=jnp.float32
        ).astype(jnp.bfloat16)
        smoothed = jnp.einsum(
            "aqp,aqc->apc", inv_factor, whitened, preferred_element_type=jnp.float32
        ).astype(jnp.bfloat16)
        projected = jnp.einsum(
            "apk,apc->akc", coupling_panel, smoothed, preferred_element_type=jnp.float32
        ).astype(jnp.bfloat16)
        projected = projected.reshape(entries, block_rows, rhs_count)
        returning = (
            jnp.zeros((device_count * slot_count, block_rows, rhs_count), jnp.bfloat16)
            .at[slot_mine]
            .set(projected)
        )
        came_back = trade_back(returning)
        summed = jnp.einsum("sb,src->brc", selector, came_back, preferred_element_type=jnp.float32)
        image_vec = prior_diag[:, :, None] * direction + summed
        curv_gram = lax.psum(inner_gram(direction, image_vec), ("arc", "vec"))
        factor_low = jnp.linalg.cholesky(curv_gram)
        step_mat = jax.scipy.linalg.cho_solve((factor_low, True), res_gram)
        solution_field = solution_field + combine_cols(direction, step_mat)
        residual = residual - combine_cols(image_vec, step_mat)
        if sweep_index + 1 < ITERS:
            new_gram = lax.psum(inner_gram(residual, residual), ("arc", "vec"))
            beta_mat = jax.scipy.linalg.cho_solve((jnp.linalg.cholesky(res_gram), True), new_gram)
            direction = residual + combine_cols(direction, beta_mat)
            res_gram = new_gram
    return (solution_field, residual)


def solution(mesh):
    in_specs = (
        P(("arc", "vec"), None, None),
        P(("arc", "vec"), None),
        P(("arc", "vec"), None, None),
        P(("arc", "vec"), None, None),
        P(),
        P(),
    )
    out_specs = (P(("arc", "vec"), None, None), P(("arc", "vec"), None, None))
    return jax.shard_map(
        per_device, mesh=mesh, in_specs=in_specs, out_specs=out_specs, check_vma=False
    )
```

profile of v0, /device:TPU:1, one launch (start us, length us, event | category | flops | bytes accessed | tf_op | source)
XLA Modules:
  0.0 1105.9 jit_solution(6747091864298645977)
XLA Ops:
  17.7 8.3 gather_fusion
  26.0 7.2 broadcast_select_fusion.1
  33.3 12.3 %all-to-all-start = ((bf16[256,128,128]{2,1,0:T(8,128)(2,1)}), bf16[256,128,128]{2,1,0:T(8,128)(2,1)}, u32[]{:S(2)}, u32[]{:S(2)}) async-start(bf16[256,128,128]{2,1,0:T(8,128)(2,1)} %broadcast_select_fusion.1), calls=%async_computation | async-start | bytes 16777216 | tf_op jit(solution)/shard_map/all_to_all | solution.py:18
  45.7 106.4 %all-to-all-done = bf16[256,128,128]{2,1,0:T(8,128)(2,1)} async-done(((bf16[256,128,128]{2,1,0:T(8,128)(2,1)}), bf16[256,128,128]{2,1,0:T(8,128)(2,1)}, u32[]{:S(2)}, u32[]{:S(2)}) %all-to-all-start) | async-done | bytes 8388640 | tf_op jit(solution)/shard_map/all_to_all | solution.py:18
  152.0 6.4 gather_fusion.1
  158.5 8.2 convolution_convert_fusion.4
  166.7 6.9 convert_bitcast_fusion.1
  173.6 6.4 copy.140
  180.0 5.3 broadcast.116.clone
  185.3 19.4 %scatter_fusion = bf16[256,128,128]{2,1,0:T(8,128)(2,1)} fusion(bf16[256,128,128]{2,1,0:T(8,128)(2,1)} %broadcast.116.clone, s32[128]{0:T(128)S(1)} %fusion.34, bf16[128,128,128]{2,1,0:T(8,128)(2,1)} %bitcast.106), kind=kCustom, calls=%fused_computation.4 | custom fusion | bytes 12583424 | tf_op jit(solution)/shard_map/scatter | solution.py:82
  204.7 6.8 all-to-all-start.1
  213.2 104.7 %all-to-all-done.1 = bf16[256,128,128]{2,1,0:T(8,128)(2,1)} async-done(((bf16[256,128,128]{2,1,0:T(8,128)(2,1)}), bf16[256,128,128]{2,1,0:T(8,128)(2,1)}, u32[]{:S(2)}, u32[]{:S(2)}) %all-to-all-start.1) | async-done | bytes 8388640 | tf_op jit(solution)/shard_map/all_to_all | solution.py:22
  317.9 7.8 fusion.2
  327.5 139.7 %all-reduce.9.cloned.1.call-done = (f32[128,128]{0,1:T(8,128)}, f32[128,128]{0,1:T(8,128)}) async-done(((f32[128,128]{0,1:T(8,128)}, f32[128,128]{0,1:T(8,128)}), (f32[128,128]{0,1:T(8,128)}, f32[128,128]{0,1:T(8,128)})) %all-reduce.9.cloned.1.call-update) | async-done | bytes 131088 | tf_op jit(solution)/shard_map/psum | solution.py:58
  470.0 11.7 %cholesky.70 = f32[128,128]{1,0:T(8,128)S(1)} custom-call(f32[128,128]{1,0:T(8,128)S(1)} %get-tuple-element.18), custom_call_target="Cholesky" | custom-call | tf_op jit(solution)/shard_map/jit(cholesky)/cholesky | solution.py:94
  482.4 11.7 %cholesky.59 = f32[128,128]{1,0:T(8,128)S(1)} custom-call(f32[128,128]{1,0:T(8,128)S(1)} %get-tuple-element.19), custom_call_target="Cholesky" | custom-call | tf_op jit(solution)/shard_map/jit(cholesky)/cholesky | solution.py:88
  495.5 9.8 custom-call.9
  508.4 10.2 all-reduce.7.cloned.1.call-start
  520.1 9.8 custom-call.10
  530.0 114.2 %all-reduce.5.cloned.1.call-done = f32[128,128]{1,0:T(8,128)} async-done(((f32[128,128]{1,0:T(8,128)}), f32[128,128]{1,0:T(8,128)}) %all-reduce.5.cloned.1.call-update) | async-done | bytes 65552 | tf_op jit(solution)/shard_map/psum | solution.py:93
  646.0 8.3 gather_fusion.2
  654.4 7.2 broadcast_select_fusion
  661.6 103.7 %all_to_all.20 = bf16[256,128,128]{2,1,0:T(8,128)(2,1)} all-to-all(bf16[256,128,128]{2,1,0:T(8,128)(2,1)} %broadcast_select_fusion), channel_id=1, replica_groups=mesh['arc'=16,'vec'=8] {'arc','vec'}, dimensions={0} | all-to-all | bytes 16777216 | tf_op jit(solution)/shard_map/all_to_all | solution.py:18
  765.3 6.4 gather_fusion.3
  771.8 9.2 convolution_convert_fusion.1
  781.0 7.2 convert_bitcast_fusion
  788.2 6.4 copy.153
  799.9 19.4 %scatter_fusion.1 = bf16[256,128,128]{2,1,0:T(8,128)(2,1)} fusion(bf16[256,128,128]{2,1,0:T(8,128)(2,1)} %broadcast.116, s32[128]{0:T(128)S(1)} %fusion.34, bf16[128,128,128]{2,1,0:T(8,128)(2,1)} %bitcast.105), kind=kCustom, calls=%fused_computation.5 | custom fusion | bytes 12583424 | tf_op jit(solution)/shard_map/scatter | solution.py:82
  819.3 106.0 %all_to_all.21 = bf16[256,128,128]{2,1,0:T(8,128)(2,1)S(1)} all-to-all(bf16[256,128,128]{2,1,0:T(8,128)(2,1)} %scatter_fusion.1), channel_id=1, replica_groups=mesh['arc'=16,'vec'=8] {'arc','vec'}, dimensions={0} | all-to-all | bytes 16777216 | tf_op jit(solution)/shard_map/all_to_all | solution.py:22
  933.2 136.1 %all-reduce.7.cloned.1.call-done = f32[128,128]{0,1:T(8,128)} async-done(((f32[128,128]{0,1:T(8,128)}), f32[128,128]{0,1:T(8,128)}) %all-reduce.7.cloned.1.call-update) | async-done | bytes 65552 | tf_op jit(solution)/shard_map/psum | solution.py:87
  1071.1 11.7 %cholesky.81 = f32[128,128]{1,0:T(8,128)S(1)} custom-call(f32[128,128]{1,0:T(8,128)S(1)} %fusion.17), custom_call_target="Cholesky" | custom-call | tf_op jit(solution)/shard_map/jit(cholesky)/cholesky | solution.py:88
  1084.2 9.8 custom-call.11
  (68 shorter events, 46.7 us)
Async XLA Ops:
  7.2 151.3 %copy-start = (bf16[16,256,256]{2,1,0:T(8,128)(2,1)S(1)}, bf16[16,256,256]{2,1,0:T(8,128)(2,1)}, u32[]{:S(2)}) copy-start(bf16[16,256,256]{2,1,0:T(8,128)(2,1)} %param.11) | copy-start | bytes 6291460
  33.3 118.8 %all-to-all-start = ((bf16[256,128,128]{2,1,0:T(8,128)(2,1)}), bf16[256,128,128]{2,1,0:T(8,128)(2,1)}, u32[]{:S(2)}, u32[]{:S(2)}) async-start(bf16[256,128,128]{2,1,0:T(8,128)(2,1)} %broadcast_select_fusion.1), calls=%async_computation | async-start | bytes 16777216 | tf_op jit(solution)/shard_map/all_to_all | solution.py:18
  204.7 7.2 copy-start.1
  204.7 113.2 %all-to-all-start.1 = ((bf16[256,128,128]{2,1,0:T(8,128)(2,1)}), bf16[256,128,128]{2,1,0:T(8,128)(2,1)}, u32[]{:S(2)}, u32[]{:S(2)}) async-start(bf16[256,128,128]{2,1,0:T(8,128)(2,1)} %scatter_fusion), calls=%async_computation.1 | async-start | bytes 16777216 | tf_op jit(solution)/shard_map/all_to_all | solution.py:22
  211.4 114.3 %copy-start.5 = (f32[5,128]{1,0:T(8,128)S(1)}, f32[5,128]{1,0:T(8,128)}, u32[]{:S(2)}) copy-start(f32[5,128]{1,0:T(8,128)} %param.10) | copy-start | bytes 7684
  211.4 255.8 %all-reduce.9.cloned.1.call-start = ((), (), s32[]{:S(2)}) async-start(), calls=%async_computation.6 | async-start | bytes 262144 | tf_op jit(solution)/shard_map/psum | solution.py:58
  327.2 317.0 %all-reduce.5.cloned.1.call-start = ((), (), s32[]{:S(2)}) async-start(), calls=%async_computation.4 | async-start | bytes 131072 | tf_op jit(solution)/shard_map/psum | solution.py:93
  481.7 13.1 %copy-start.4 = (f32[128,128]{1,0:T(8,128)}, f32[128,128]{1,0:T(8,128)S(1)}, u32[]{:S(2)}) copy-start(f32[128,128]{1,0:T(8,128)S(1)} %cholesky.70) | copy-start | bytes 196612
  508.4 560.9 %all-reduce.7.cloned.1.call-start = ((), (), s32[]{:S(2)}) async-start(), calls=%async_computation.5 | async-start | bytes 131072 | tf_op jit(solution)/shard_map/psum | solution.py:87
  925.3 168.7 %copy-start.3 = (f32[128,128]{1,0:T(8,128)S(1)}, f32[128,128]{1,0:T(8,128)}, u32[]{:S(2)}) copy-start(f32[128,128]{1,0:T(8,128)} %all-reduce.5.cloned.1.call-done) | copy-start | bytes 196612
  929.7 0.8 copy-start.2
Sparse Core Ops, SparseCore 0:
  327.3 139.8 all-reduce.8
  508.6 135.5 all-reduce.4
  932.1 137.1 all-reduce.6
where the time goes:
time: 1110 us
  waiting for transfers between devices  601 us (54%)
  blocking collectives  210 us (19%)
  local copies, waits for them, and re-layouts  100 us (9%)
  other arithmetic  92 us (8%)
  matrix products  58.4 us (5%)
  starting transfers between devices  29.9 us (3%)
  between operations  14.3 us (1%)
    psum x1, waiting for transfers between devices, per_device(): res_gram = lax.psum(inner_gram(residual, residual), ('arc', 'vec'))  140 us
    psum x1, waiting for transfers between devices, per_device(): curv_gram = lax.psum(inner_gram(direction, image_vec), ('arc', 'vec'))  136 us
    psum x1, waiting for transfers between devices, per_device(): new_gram = lax.psum(inner_gram(residual, residual), ('arc', 'vec'))  114 us
    all_to_all x1, waiting for transfers between devices, trade_out(): lax.all_to_all(buffer, ('arc', 'vec'), split_axis=0, concat_axis=0, tiled...  106 us
    all_to_all x1, blocking collectives, trade_back(): lax.all_to_all(buffer, ('arc', 'vec'), split_axis=0, concat_axis=0, tiled...  106 us
    all_to_all x1, waiting for transfers between devices, trade_back(): lax.all_to_all(buffer, ('arc', 'vec'), split_axis=0, concat_axis=0, tiled...  105 us
    all_to_all x1, blocking collectives, trade_out(): lax.all_to_all(buffer, ('arc', 'vec'), split_axis=0, concat_axis=0, tiled...  104 us
    scatter x2, local copies, waits for them, and re-layouts, per_device(): returning = jnp.zeros((device_count * slot_count, block_rows, rhs_count),...  38.7 us
  transfers between devices with their start and end apart: 5, of which 5 were waited for; matrix products, arithmetic and copies ran while one was open for 1% of the time, Pallas kernels for 0%

commit v1 on v0

--- a/solution.py
+++ b/solution.py
@@ -55,7 +55,7 @@
     solution_field = jnp.zeros_like(right_side)
     residual = right_side
     direction = right_side
-    res_gram = lax.psum(inner_gram(residual, residual), ("arc", "vec"))
+    res_gram = lax.psum(lax.psum(inner_gram(residual, residual), "arc"), "vec")
     for sweep_index in range(ITERS):
         local_rounded = direction.astype(jnp.bfloat16)
         outgoing = jnp.where(

time: 1110 us -> 1220 us (1.099)
  waiting for transfers between devices: 601 us -> 718 us
    psum x1 -> x2, waiting for transfers between devices: 136 us -> 273 us  [per_device(): curv_gram = lax.psum(inner_gram(direction, image_vec), ('arc', 'vec'))]
    all_to_all x1, waiting for transfers between devices: 105 us -> 0.01 us  [trade_back(): lax.all_to_all(buffer, ('arc', 'vec'), split_axis=0, concat_axis=0, tiled...]
    psum x1 -> x2, waiting for transfers between devices: 140 us -> 216 us  [per_device(): res_gram = lax.psum(lax.psum(inner_gram(residual, residual), 'arc'), 'vec')]
  transfers between devices with their start and end apart: 5 -> 7, of which waited for: 5 -> 6; matrix products, arithmetic and copies ran while one was open for 1% -> 2% of each run, Pallas kernels for 0% -> 0%
where the time goes in v1:
time: 1220 us
  waiting for transfers between devices  718 us (59%)
  blocking collectives  211 us (17%)
  local copies, waits for them, and re-layouts  100 us (8%)
  other arithmetic  92.8 us (8%)
  matrix products  57.6 us (5%)
  starting transfers between devices  20.3 us (2%)
  between operations  16.2 us (1%)
    psum x2, waiting for transfers between devices, per_device(): curv_gram = lax.psum(inner_gram(direction, image_vec), ('arc', 'vec'))  273 us
    psum x2, waiting for transfers between devices, per_device(): res_gram = lax.psum(lax.psum(inner_gram(residual, residual), 'arc'), 'vec')  216 us
    psum x1, waiting for transfers between devices, per_device(): new_gram = lax.psum(inner_gram(residual, residual), ('arc', 'vec'))  123 us
    all_to_all x1, blocking collectives, trade_back(): lax.all_to_all(buffer, ('arc', 'vec'), split_axis=0, concat_axis=0, tiled...  107 us
    all_to_all x1, waiting for transfers between devices, trade_out(): lax.all_to_all(buffer, ('arc', 'vec'), split_axis=0, concat_axis=0, tiled...  106 us
    all_to_all x1, blocking collectives, trade_out(): lax.all_to_all(buffer, ('arc', 'vec'), split_axis=0, concat_axis=0, tiled...  104 us
    scatter x2, local copies, waits for them, and re-layouts, per_device(): returning = jnp.zeros((device_count * slot_count, block_rows, rhs_count),...  38.6 us
    another operation x6, other arithmetic, per_device(): factor_low = jnp.linalg.cholesky(curv_gram)  24.8 us
  transfers between devices with their start and end apart: 7, of which 6 were waited for; matrix products, arithmetic and copies ran while one was open for 2% of the time, Pallas kernels for 0%

profile of v1, /device:TPU:1, one launch (start us, length us, event | category | flops | bytes accessed | tf_op | source)
XLA Modules:
  0.0 1216.3 jit_solution(4934429302587030647)
XLA Ops:
  18.5 8.3 gather_fusion
  26.9 7.2 broadcast_select_fusion.1
  34.1 12.3 %all-to-all-start = ((bf16[256,128,128]{2,1,0:T(8,128)(2,1)}), bf16[256,128,128]{2,1,0:T(8,128)(2,1)}, u32[]{:S(2)}, u32[]{:S(2)}) async-start(bf16[256,128,128]{2,1,0:T(8,128)(2,1)} %broadcast_select_fusion.1), calls=%async_computation | async-start | bytes 16777216 | tf_op jit(solution)/shard_map/all_to_all | solution.py:18
  46.5 106.4 %all-to-all-done = bf16[256,128,128]{2,1,0:T(8,128)(2,1)} async-done(((bf16[256,128,128]{2,1,0:T(8,128)(2,1)}), bf16[256,128,128]{2,1,0:T(8,128)(2,1)}, u32[]{:S(2)}, u32[]{:S(2)}) %all-to-all-start) | async-done | bytes 8388640 | tf_op jit(solution)/shard_map/all_to_all | solution.py:18
  152.9 6.4 gather_fusion.1
  159.3 8.2 convolution_convert_fusion.4
  167.5 6.9 convert_bitcast_fusion.1
  174.5 6.4 copy.140
  186.2 19.3 %scatter_fusion = bf16[256,128,128]{2,1,0:T(8,128)(2,1)} fusion(bf16[256,128,128]{2,1,0:T(8,128)(2,1)} %broadcast.116.clone, s32[128]{0:T(128)S(1)} %fusion.34, bf16[128,128,128]{2,1,0:T(8,128)(2,1)} %bitcast.106), kind=kCustom, calls=%fused_computation.4 | custom fusion | bytes 12583424 | tf_op jit(solution)/shard_map/scatter | solution.py:82
  205.5 6.8 all-to-all-start.1
  213.8 156.3 %all-reduce.8.cloned.1.call-done = f32[128,128]{0,1:T(8,128)} async-done(((f32[128,128]{0,1:T(8,128)}), f32[128,128]{0,1:T(8,128)}) %all-reduce.8.cloned.1.call-update) | async-done | bytes 65552 | tf_op jit(solution)/shard_map/psum | solution.py:58
  370.5 59.5 %all-reduce.10.cloned.1.call-done = f32[128,128]{0,1:T(8,128)} async-done(((f32[128,128]{0,1:T(8,128)}), f32[128,128]{0,1:T(8,128)}) %all-reduce.10.cloned.1.call-update) | async-done | bytes 65552 | tf_op jit(solution)/shard_map/psum | solution.py:58
  431.9 11.7 cholesky.70
  443.6 7.8 fusion.2
  453.9 137.6 %all-reduce.6.cloned.1.call-done = f32[128,128]{0,1:T(8,128)} async-done(((f32[128,128]{0,1:T(8,128)}), f32[128,128]{0,1:T(8,128)}) %all-reduce.6.cloned.1.call-update) | async-done | bytes 65552 | tf_op jit(solution)/shard_map/psum | solution.py:87
  593.3 11.7 cholesky.59
  606.3 9.8 custom-call.9
  620.5 9.8 custom-call.10
  630.3 122.7 %all-reduce.12.cloned.1.call-done = f32[128,128]{1,0:T(8,128)} async-done(((f32[128,128]{1,0:T(8,128)}), f32[128,128]{1,0:T(8,128)}) %all-reduce.12.cloned.1.call-update) | async-done | bytes 65552 | tf_op jit(solution)/shard_map/psum | solution.py:93
  754.8 8.3 gather_fusion.2
  763.2 7.2 broadcast_select_fusion
  770.4 103.9 %all_to_all.20 = bf16[256,128,128]{2,1,0:T(8,128)(2,1)} all-to-all(bf16[256,128,128]{2,1,0:T(8,128)(2,1)} %broadcast_select_fusion), channel_id=1, replica_groups=mesh['arc'=16,'vec'=8] {'arc','vec'}, dimensions={0} | all-to-all | bytes 16777216 | tf_op jit(solution)/shard_map/all_to_all | solution.py:18
  874.3 6.4 gather_fusion.3
  880.7 9.2 convolution_convert_fusion.1
  890.0 7.2 convert_bitcast_fusion
  897.2 6.4 copy.153
  903.5 5.3 broadcast.116
  908.9 19.4 %scatter_fusion.1 = bf16[256,128,128]{2,1,0:T(8,128)(2,1)} fusion(bf16[256,128,128]{2,1,0:T(8,128)(2,1)} %broadcast.116, s32[128]{0:T(128)S(1)} %fusion.34, bf16[128,128,128]{2,1,0:T(8,128)(2,1)} %bitcast.105), kind=kCustom, calls=%fused_computation.5 | custom fusion | bytes 12583424 | tf_op jit(solution)/shard_map/scatter | solution.py:82
  928.2 106.9 %all_to_all.21 = bf16[256,128,128]{2,1,0:T(8,128)(2,1)S(1)} all-to-all(bf16[256,128,128]{2,1,0:T(8,128)(2,1)} %scatter_fusion.1), channel_id=1, replica_groups=mesh['arc'=16,'vec'=8] {'arc','vec'}, dimensions={0} | all-to-all | bytes 16777216 | tf_op jit(solution)/shard_map/all_to_all | solution.py:22
  1043.1 135.7 %all-reduce.14.cloned.1.call-done = f32[128,128]{0,1:T(8,128)} async-done(((f32[128,128]{0,1:T(8,128)}), f32[128,128]{0,1:T(8,128)}) %all-reduce.14.cloned.1.call-update) | async-done | bytes 65552 | tf_op jit(solution)/shard_map/psum | solution.py:87
  1180.5 11.7 cholesky.81
  1193.6 9.8 custom-call.11
  (77 shorter events, 47.3 us)
Async XLA Ops:
  8.0 151.3 %copy-start = (bf16[16,256,256]{2,1,0:T(8,128)(2,1)S(1)}, bf16[16,256,256]{2,1,0:T(8,128)(2,1)}, u32[]{:S(2)}) copy-start(bf16[16,256,256]{2,1,0:T(8,128)(2,1)} %param.11) | copy-start | bytes 6291460
  34.1 118.8 %all-to-all-start = ((bf16[256,128,128]{2,1,0:T(8,128)(2,1)}), bf16[256,128,128]{2,1,0:T(8,128)(2,1)}, u32[]{:S(2)}, u32[]{:S(2)}) async-start(bf16[256,128,128]{2,1,0:T(8,128)(2,1)} %broadcast_select_fusion.1), calls=%async_computation | async-start | bytes 16777216 | tf_op jit(solution)/shard_map/all_to_all | solution.py:18
  205.5 6.9 copy-start.1
  205.5 238.1 %all-to-all-start.1 = ((bf16[256,128,128]{2,1,0:T(8,128)(2,1)}), bf16[256,128,128]{2,1,0:T(8,128)(2,1)}, u32[]{:S(2)}, u32[]{:S(2)}) async-start(bf16[256,128,128]{2,1,0:T(8,128)(2,1)} %scatter_fusion), calls=%async_computation.1 | async-start | bytes 16777216 | tf_op jit(solution)/shard_map/all_to_all | solution.py:22
  212.3 239.2 %copy-start.6 = (f32[5,128]{1,0:T(8,128)S(1)}, f32[5,128]{1,0:T(8,128)}, u32[]{:S(2)}) copy-start(f32[5,128]{1,0:T(8,128)} %param.10) | copy-start | bytes 7684
  212.3 157.8 %all-reduce.8.cloned.1.call-start = ((), (), s32[]{:S(2)}) async-start(), calls=%async_computation.5 | async-start | bytes 131072 | tf_op jit(solution)/shard_map/psum | solution.py:58
  213.7 216.3 %all-reduce.10.cloned.1.call-start = ((), (), s32[]{:S(2)}) async-start(), calls=%async_computation.6 | async-start | bytes 131072 | tf_op jit(solution)/shard_map/psum | solution.py:58
  370.1 221.4 %all-reduce.6.cloned.1.call-start = ((), (), s32[]{:S(2)}) async-start(), calls=%async_computation.4 | async-start | bytes 131072 | tf_op jit(solution)/shard_map/psum | solution.py:87
  430.0 186.2 %copy-start.3 = (f32[128,128]{0,1:T(8,128)S(1)}, f32[128,128]{0,1:T(8,128)}, u32[]{:S(2)}) copy-start(f32[128,128]{0,1:T(8,128)} %all-reduce.10.cloned.1.call-done) | copy-start | bytes 196612
  443.6 10.3 copy-start.5
  452.9 300.0 %all-reduce.12.cloned.1.call-start = ((), (), s32[]{:S(2)}) async-start(), calls=%async_computation.7 | async-start | bytes 131072 | tf_op jit(solution)/shard_map/psum | solution.py:93
  618.5 560.2 %all-reduce.14.cloned.1.call-start = ((), (), s32[]{:S(2)}) async-start(), calls=%async_computation.8 | async-start | bytes 131072 | tf_op jit(solution)/shard_map/psum | solution.py:87
  1035.1 168.3 %copy-start.4 = (f32[128,128]{1,0:T(8,128)S(1)}, f32[128,128]{1,0:T(8,128)}, u32[]{:S(2)}) copy-start(f32[128,128]{1,0:T(8,128)} %all-reduce.12.cloned.1.call-done) | copy-start | bytes 196612
  1039.6 0.8 copy-start.2
Sparse Core Ops, SparseCore 0:
  216.9 153.0 all-reduce.7
  372.5 57.4 all-reduce.9
Sparse Core Ops, SparseCore 1:
  453.0 138.4 all-reduce.5
  618.6 134.3 all-reduce.11
  1041.9 136.7 all-reduce.13
